TPU v7x, 32 devices: a whole 2x2x4 slice. The times are simulated.
32 devices in a mesh: groups: 2 (over y), tensor: 4 (over z), dp: 4 (over x, core).
Axes of the slice: x: 2, y: 2, z: 4, core: 2. Of those that a mesh axis runs over, the one named last changes fastest.
Arguments:
- tokens: bfloat16 [256, 8192], P(('groups', 'tensor', 'dp')), parts along dimension 0, may hold values from -6 to 6
- gate_projection_matrix: bfloat16 [8192, 14336], P('dp', 'tensor'), may hold values from -0.0625 to 0.0625
- up_projection_matrix: bfloat16 [8192, 14336], P('dp', 'tensor'), may hold values from -0.0625 to 0.0625
- down_projection_matrix: bfloat16 [14336, 8192], P('tensor', 'dp'), may hold values from -0.046875 to 0.046875
- gate_adapter_inmap: bfloat16 [16384, 64], P(('groups', 'dp')), parts along dimension 0, may hold values from -0.0625 to 0.0625
- gate_adapter_outmap: bfloat16 [64, 28672], P(None, ('groups', 'tensor')), parts along dimension 1, may hold values from -0.75 to 0.75
- up_adapter_inmap: bfloat16 [16384, 64], P(('groups', 'dp')), parts along dimension 0, may hold values from -0.0625 to 0.0625
- up_adapter_outmap: bfloat16 [64, 28672], P(None, ('groups', 'tensor')), parts along dimension 1, may hold values from -0.75 to 0.75
- down_adapter_inmap: bfloat16 [28672, 64], P(('groups', 'tensor')), parts along dimension 0, may hold values from -0.046875 to 0.046875
- down_adapter_outmap: bfloat16 [64, 16384], P(None, 'groups'), parts along dimension 1, may hold values from -0.75 to 0.75
Outputs:
- block_out: bfloat16 [256, 8192], P(('groups', 'tensor', 'dp')), parts along dimension 0
There are 2 independent parts, one for each index of `groups`. A program takes and returns all parts, laid end to end along the dimension named above; an argument that names none is the same for every part. Nothing has to cross between parts.
All inputs are finite; a program needn't handle non-finite values.
Results may differ from a plain program's by a relative error of at most 0.0053.
Values may be sent and summed in bfloat16 or wider, within the bound.
A program may use at most 256 MiB of HBM per device.

v0:
```python
import jax
import jax.numpy as jnp
from jax import lax
from jax.sharding import PartitionSpec as P

adapter_scale_factor = 0.5


def body(
    tokens,
    gate_projection_matrix,
    up_projection_matrix,
    down_projection_matrix,
    gate_adapter_inmap,
    gate_adapter_outmap,
    up_adapter_inmap,
    up_adapter_outmap,
    down_adapter_inmap,
    down_adapter_outmap,
):
    tok_dev = tokens.shape[0]
    n_tensor = lax.axis_size("tensor")
    n_dp = lax.axis_size("dp")
    hidden_unit_count = gate_projection_matrix.shape[1]
    adapter_rank_size = gate_adapter_inmap.shape[1]
    columns = lax.all_to_all(tokens, "dp", split_axis=1, concat_axis=0, tiled=True)
    stacked_lowrank = jnp.concatenate(
        [gate_projection_matrix, up_projection_matrix, gate_adapter_inmap, up_adapter_inmap], axis=1
    )
    partial_all = jnp.dot(
        lax.all_gather(columns, "tensor", axis=0, tiled=True),
        stacked_lowrank,
        preferred_element_type=jnp.float32,
    )
    partial_all = partial_all.reshape(n_tensor, n_dp, tok_dev, partial_all.shape[1])
    summed_lowrank = lax.psum_scatter(partial_all, "dp", scatter_dimension=1, tiled=True)
    summed_lowrank = summed_lowrank.reshape(n_tensor * tok_dev, summed_lowrank.shape[3])
    gate_dense_part = summed_lowrank[:, :hidden_unit_count]
    up_dense_part = summed_lowrank[:, hidden_unit_count : 2 * hidden_unit_count]
    gate_lowrank_part = summed_lowrank[
        :, 2 * hidden_unit_count : 2 * hidden_unit_count + adapter_rank_size
    ].astype(jnp.bfloat16)
    up_lowrank_part = summed_lowrank[:, 2 * hidden_unit_count + adapter_rank_size :].astype(
        jnp.bfloat16
    )
    gate_activated = gate_dense_part + adapter_scale_factor * jnp.dot(
        gate_lowrank_part, gate_adapter_outmap, preferred_element_type=jnp.float32
    )
    up_projected_value = up_dense_part + adapter_scale_factor * jnp.dot(
        up_lowrank_part, up_adapter_outmap, preferred_element_type=jnp.float32
    )
    hidden_product = (jax.nn.silu(gate_activated) * up_projected_value).astype(jnp.bfloat16)
    down_outmap_single = down_adapter_outmap.astype(jnp.float32)
    lowrank_term_list = jnp.dot(
        hidden_product, down_adapter_inmap, preferred_element_type=jnp.float32
    )
    owned_lowrank_part = lax.psum_scatter(
        lowrank_term_list, "tensor", scatter_dimension=0, tiled=True
    )
    term = jnp.dot(
        hidden_product,
        lax.all_gather(down_projection_matrix, "dp", axis=1, tiled=True),
        preferred_element_type=jnp.float32,
    )
    block_result_rows = lax.psum_scatter(term, "tensor", scatter_dimension=0, tiled=True)
    block_result_rows = block_result_rows + adapter_scale_factor * jnp.dot(
        owned_lowrank_part, down_outmap_single, precision=lax.Precision.HIGHEST
    )
    return block_result_rows.astype(jnp.bfloat16)


def solution(mesh):
    placed = (
        P(("groups", "tensor", "dp"), None),
        P("dp", "tensor"),
        P("dp", "tensor"),
        P("tensor", "dp"),
        P(("groups", "dp"), None),
        P(None, ("groups", "tensor")),
        P(("groups", "dp"), None),
        P(None, ("groups", "tensor")),
        P(("groups", "tensor"), None),
        P(None, "groups"),
    )
    return jax.shard_map(
        body,
        mesh=mesh,
        in_specs=placed,
        out_specs=P(("groups", "tensor", "dp"), None),
        check_vma=False,
    )
```

profile of v0, /device:TPU:0, one launch (start us, length us, event | category | flops | bytes accessed | tf_op | source)
XLA Modules:
  0.0 576.1 jit_solution(376535880790217102)
XLA Ops:
  6.5 0.0 copy-start
  6.5 4.4 all-to-all-start
  10.9 0.0 all-reduce.4.cloned.1.call-start
  10.9 1.2 copy.13
  12.1 1.2 copy.14
  13.4 44.4 %concatenate.3 = bf16[2048,7296]{1,0:T(8,128)(2,1)} concatenate(bf16[2048,3584]{1,0:T(8,128)(2,1)} %param.11, bf16[2048,3584]{1,0:T(8,128)(2,1)} %param.12, bf16[2048,64]{1,0:T(8,128)(2,1)S(1)} %copy.13, bf16[2048,64]{1,0:T(8,128)(2,1)S(1)} %copy.14), dimensions={1} | concatenate | bytes 59768832 | tf_op jit(solution)/shard_map/concatenate | solution.py:27
  57.7 0.0 copy-start.5
  57.8 0.0 copy-start.2
  57.8 0.0 copy-start.3
  57.8 0.0 all-to-all-done
  57.8 17.1 %all_gather.6 = bf16[128,2048]{1,0:T(8,128)(2,1)S(1)} all-gather(bf16[32,2048]{1,0:T(8,128)(2,1)S(1)} %bitcast.24), channel_id=1, replica_groups=mesh['groups'=2,'tensor'=4,'dp'=4] {'tensor'}, dimensions={0}, use_global_device_ids=true | all-gather | bytes 655360 | tf_op jit(solution)/shard_map/all_gather | solution.py:31
  74.9 15.4 %fusion.13 = f32[7296,128]{0,1:T(8,128)} fusion(bf16[128,2048]{1,0:T(8,128)(2,1)S(1)} %all_gather.6, bf16[2048,7296]{1,0:T(8,128)(2,1)} %concatenate.3), kind=kOutput, calls=%fused_computation.17 | convolution fusion | flops 3825205248 | bytes 34144256 | tf_op jit(solution)/shard_map/dot_general | solution.py:30
  90.3 0.0 all-reduce.4.cloned.1.call-update
  90.3 0.0 all-gather.2.cloned.1.call-start
  90.4 0.7 all-gather.2.cloned.1.call-update
  91.1 0.0 reduce-scatter.3.cloned.1.call-start
  91.2 0.0 copy-done.5
  91.2 0.6 dynamic-slice
  91.7 78.5 %all-reduce.4.cloned.1.call-done = f32[4,4,8,7296]{3,2,1,0:T(8,128)} async-done(((f32[4,4,8,7296]{3,2,1,0:T(8,128)}), f32[4,4,8,7296]{3,2,1,0:T(8,128)}) %all-reduce.4.cloned.1.call-update) | async-done | bytes 3735568
  170.2 1.9 fusion.10
  172.2 0.0 copy-done.2
  172.2 0.2 fusion.4
  172.4 0.0 copy-done.3
  172.4 0.3 fusion.5
  172.7 0.0 copy-start.4
  172.7 0.0 copy-start.1
  172.7 345.2 %all-gather.2.cloned.1.call-done = bf16[3584,8192]{1,0:T(8,128)(2,1)} async-done(((bf16[3584,2048]{1,0:T(8,128)(2,1)}), bf16[3584,8192]{1,0:T(8,128)(2,1)}) %all-gather.2.cloned.1.call-update) | async-done | bytes 58720272 | tf_op jit(solution)/shard_map/all_gather | solution.py:62
  518.0 21.6 %fusion.11 = f32[32,8192]{1,0:T(8,128)} fusion(bf16[32,3584]{1,0:T(8,128)(2,1)S(1)} %fusion.5, bf16[3584,8192]{1,0:T(8,128)(2,1)} %all-gather.2.cloned.1.call-done), kind=kOutput, calls=%fused_computation.15 | convolution fusion | flops 1879048192 | bytes 59998208 | tf_op jit(solution)/shard_map/dot_general | solution.py:60
  539.6 0.0 reduce-scatter.3.cloned.1.call-update
  539.6 0.0 copy-done.4
  539.6 0.6 dynamic-slice.2
  540.9 0.0 copy-done.1
  540.9 0.2 fusion.12
  541.1 19.7 %all-reduce.1 = f32[32,64]{1,0:T(8,128)S(1)} all-reduce(f32[32,64]{1,0:T(8,128)S(1)} %fusion.12), channel_id=4, replica_groups=mesh['groups'=2,'tensor'=4,'dp'=4] {'tensor'}, use_global_device_ids=true, to_apply=%region_2.3.clone | all-reduce | flops 2048 | bytes 16384
  560.9 6.6 %reduce-scatter.3.cloned.1.call-done = f32[8,8192]{1,0:T(8,128)} async-done(((f32[32,8192]{1,0:T(8,128)}), f32[8,8192]{1,0:T(8,128)}) %reduce-scatter.3.cloned.1.call-update) | async-done | bytes 262160 | tf_op jit(solution)/shard_map/reduce_scatter | solution.py:65
  567.4 0.0 copy-done
  567.4 2.1 fusion.1
Async XLA Ops:
  6.5 560.9 %copy-start = (bf16[64,8192]{1,0:T(8,128)(2,1)S(1)}, bf16[64,8192]{1,0:T(8,128)(2,1)}, u32[]{:S(2)}) copy-start(bf16[64,8192]{1,0:T(8,128)(2,1)} %param.19) | copy-start | bytes 3145732
  6.5 51.2 %all-to-all-start = ((bf16[8,4,2048]{2,0,1:T(8,128)(2,1)}), bf16[8,4,2048]{2,0,1:T(8,128)(2,1)S(1)}, u32[]{:S(2)}, u32[]{:S(2)}) async-start(bf16[8,4,2048]{2,0,1:T(8,128)(2,1)} %bitcast.25), calls=%async_computation | async-start | bytes 262144 | tf_op jit(solution)/shard_map/all_to_all | solution.py:26
  10.9 159.3 %all-reduce.4.cloned.1.call-start = ((), (), s32[]{:S(2)}) async-start(), calls=%async_computation.4 | async-start | bytes 7471104
  57.7 33.4 %copy-start.5 = (u32[32]{0:T(128)S(1)}, u32[32]{0:T(128)}, u32[]{:S(2)}) copy-start(u32[32]{0:T(128)} %constant.9) | copy-start | bytes 388
  57.8 114.4 %copy-start.2 = (bf16[64,3584]{1,0:T(8,128)(2,1)S(1)}, bf16[64,3584]{1,0:T(8,128)(2,1)}, u32[]{:S(2)}) copy-start(bf16[64,3584]{1,0:T(8,128)(2,1)} %param.15) | copy-start | bytes 1376260
  57.8 114.6 %copy-start.3 = (bf16[64,3584]{1,0:T(8,128)(2,1)S(1)}, bf16[64,3584]{1,0:T(8,128)(2,1)}, u32[]{:S(2)}) copy-start(bf16[64,3584]{1,0:T(8,128)(2,1)} %param.17) | copy-start | bytes 1376260
  90.3 427.6 %all-gather.2.cloned.1.call-start = ((), (), s32[]{:S(2)}) async-start(), calls=%async_computation.2 | async-start | bytes 73400320 | tf_op jit(solution)/shard_map/all_gather | solution.py:62
  91.1 476.3 %reduce-scatter.3.cloned.1.call-start = ((), (), s32[]{:S(2)}) async-start(), calls=%async_computation.3 | async-start | bytes 1310720 | tf_op jit(solution)/shard_map/reduce_scatter | solution.py:65
  172.7 366.9 %copy-start.4 = (u32[32]{0:T(128)S(1)}, u32[32]{0:T(128)}, u32[]{:S(2)}) copy-start(u32[32]{0:T(128)} %constant.13) | copy-start | bytes 388
  172.7 368.2 %copy-start.1 = (bf16[3584,64]{0,1:T(8,128)(2,1)S(1)}, bf16[3584,64]{0,1:T(8,128)(2,1)}, u32[]{:S(2)}) copy-start(bf16[3584,64]{0,1:T(8,128)(2,1)} %param.18) | copy-start | bytes 1376260
Sparse Core Ops, SparseCore 0:
  90.5 79.7 all-reduce.3
  171.8 346.1 all-gather.1
  539.8 27.6 reduce-scatter.2
where the time goes:
time: 578 us; the launch traced here: 576 us
  waiting for transfers between devices  431 us (75%)
  local copies, waits for them, and re-layouts  48 us (8%)
  matrix products  39.9 us (7%)
  blocking collectives  36.9 us (6%)
  between operations  13.9 us (2%)
    all_gather x1, waiting for transfers between devices, body(): lax.all_gather(down_projection_matrix, 'dp', axis=1, tiled=True)  345 us
    unnamed x4, waiting for transfers between devices  79.2 us
    concatenate x1, local copies, waits for them, and re-layouts, body(): jnp.concatenate([gate_projection_matrix, up_projection_matrix, gate_adapt...  44.4 us
    dot_general x1, matrix products, body(): jnp.dot(hidden_product, lax.all_gather(down_projection_matrix, 'dp', axis...  21.6 us
    unnamed x1, blocking collectives  19.7 us
    all_gather x1, blocking collectives, body(): lax.all_gather(columns, 'tensor', axis=0, tiled=True)  17.1 us
    dot_general x1, matrix products, body(): jnp.dot(lax.all_gather(columns, 'tensor', axis=0, tiled=True), stacked_lo...  15.4 us
  transfers between devices with their start and end apart: 4, of which 3 were waited for; matrix products, arithmetic and copies ran while one was open for 9% of the time, Pallas kernels for 0%

commit v1 on v0

--- a/solution.py
+++ b/solution.py
@@ -4,6 +4,17 @@
 from jax.sharding import PartitionSpec as P
 
 adapter_scale_factor = 0.5
+
+
+def collect(array, axis, dim):
+    ways = lax.axis_size(axis)
+    pieces = [array]
+    for far in range(1, ways):
+        pieces.append(
+            lax.ppermute(pieces[far - 1], axis, [(d, (d - 1) % ways) for d in range(ways)])
+        )
+    line = jnp.concatenate(pieces, axis=dim)
+    return jnp.roll(line, lax.axis_index(axis) * array.shape[dim], axis=dim)
 
 
 def body(
@@ -58,9 +69,7 @@
         lowrank_term_list, "tensor", scatter_dimension=0, tiled=True
     )
     term = jnp.dot(
-        hidden_product,
-        lax.all_gather(down_projection_matrix, "dp", axis=1, tiled=True),
-        preferred_element_type=jnp.float32,
+        hidden_product, collect(down_projection_matrix, "dp", 1), preferred_element_type=jnp.float32
     )
     block_result_rows = lax.psum_scatter(term, "tensor", scatter_dimension=0, tiled=True)
     block_result_rows = block_result_rows + adapter_scale_factor * jnp.dot(

time: 578 us -> 764 us (1.32)
  local copies, waits for them, and re-layouts: 48 us -> 161 us
  waiting for transfers between devices: 431 us -> 500 us
    all_gather x1 -> x0, waiting for transfers between devices: 345 us -> none  [body(): lax.all_gather(down_projection_matrix, 'dp', axis=1, tiled=True)]
    ppermute x0 -> x3, waiting for transfers between devices: none -> 317 us  [collect(): lax.ppermute(pieces[far - 1], axis, [(d, (d - 1) % ways) for d in range(w...]
    all_to_all x1, waiting for transfers between devices: 0.01 us -> 111 us  [body(): lax.all_to_all(tokens, 'dp', split_axis=1, concat_axis=0, tiled=True)]
    unnamed x16 -> x23, local copies, waits for them, and re-layouts: 3.65 us -> 104 us
    unnamed x4 -> x3, waiting for transfers between devices: 79.2 us -> 65.1 us
    concatenate x0 -> x1, local copies, waits for them, and re-layouts: none -> 13.4 us  [collect(): return jnp.roll(line, lax.axis_index(axis) * array.shape[dim], axis=dim)]
  transfers between devices with their start and end apart: 4 -> 6, of which waited for: 3 -> 5; matrix products, arithmetic and copies ran while one was open for 9% -> 14% of each run, Pallas kernels for 0% -> 0%
where the time goes in v1:
time: 764 us; the launch traced here: 762 us
  waiting for transfers between devices  500 us (65%)
  local copies, waits for them, and re-layouts  161 us (21%)
  matrix products  38.4 us (5%)
  blocking collectives  34.9 us (5%)
  between operations  14.2 us (2%)
  starting transfers between devices  9.62 us (1%)
    ppermute x3, waiting for transfers between devices, collect(): lax.ppermute(pieces[far - 1], axis, [(d, (d - 1) % ways) for d in range(w...  317 us
    all_to_all x1, waiting for transfers between devices, body(): lax.all_to_all(tokens, 'dp', split_axis=1, concat_axis=0, tiled=True)  111 us
    unnamed x23, local copies, waits for them, and re-layouts  104 us
    unnamed x3, waiting for transfers between devices  65.1 us
    concatenate x1, local copies, waits for them, and re-layouts, body(): jnp.concatenate([gate_projection_matrix, up_projection_matrix, gate_adapt...  44.4 us
    dot_general x1, matrix products, body(): jnp.dot(hidden_product, collect(down_projection_matrix, 'dp', 1), preferr...  21.7 us
    unnamed x1, blocking collectives  19.3 us
    all_gather x1, blocking collectives, body(): lax.all_gather(columns, 'tensor', axis=0, tiled=True)  15.6 us
  transfers between devices with their start and end apart: 6, of which 5 were waited for; matrix products, arithmetic and copies ran while one was open for 14% of the time, Pallas kernels for 0%

profile of v1, /device:TPU:0, one launch (start us, length us, event | category | flops | bytes accessed | tf_op | source)
XLA Modules:
  0.0 762.0 jit_solution(3875969877405818917)
XLA Ops:
  6.5 0.0 copy-start
  6.5 0.0 copy-start.3
  6.5 0.0 copy-start.4
  6.5 2.4 collective-permute-start
  8.9 158.7 %collective-permute-done = bf16[3584,2048]{1,0:T(8,128)(2,1)S(1)} collective-permute-done((bf16[3584,2048]{1,0:T(8,128)(2,1)}, bf16[3584,2048]{1,0:T(8,128)(2,1)S(1)}, u32[]{:S(2)}, u32[]{:S(2)}) %collective-permute-start) | collective-permute-done | bytes 14680096 | tf_op jit(solution)/shard_map/ppermute | solution.py:14
  167.6 0.0 copy-start.1
  167.6 5.2 copy-done.1
  172.9 1.8 collective-permute-start.1
  174.7 158.4 %collective-permute-done.1 = bf16[3584,2048]{1,0:T(8,128)(2,1)} collective-permute-done((bf16[3584,2048]{1,0:T(8,128)(2,1)S(1)}, bf16[3584,2048]{1,0:T(8,128)(2,1)}, u32[]{:S(2)}, u32[]{:S(2)}) %collective-permute-start.1) | collective-permute-done | bytes 14680096 | tf_op jit(solution)/shard_map/ppermute | solution.py:14
  333.0 2.0 collective-permute-start.2
  335.1 3.3 all-to-all-start
  338.4 0.0 all-reduce.4.cloned.1.call-start
  338.4 1.2 copy.13
  339.7 1.2 copy.14
  340.9 44.4 %concatenate.9 = bf16[2048,7296]{1,0:T(8,128)(2,1)} concatenate(bf16[2048,3584]{1,0:T(8,128)(2,1)} %param.11, bf16[2048,3584]{1,0:T(8,128)(2,1)} %param.12, bf16[2048,64]{1,0:T(8,128)(2,1)S(1)} %copy.13, bf16[2048,64]{1,0:T(8,128)(2,1)S(1)} %copy.14), dimensions={1} | concatenate | bytes 59768832 | tf_op jit(solution)/shard_map/concatenate | solution.py:38
  385.3 110.8 %all-to-all-done = bf16[8,4,2048]{2,0,1:T(8,128)(2,1)S(1)} async-done(((bf16[8,4,2048]{2,0,1:T(8,128)(2,1)}), bf16[8,4,2048]{2,0,1:T(8,128)(2,1)S(1)}, u32[]{:S(2)}, u32[]{:S(2)}) %all-to-all-start) | async-done | bytes 131104 | tf_op jit(solution)/shard_map/all_to_all | solution.py:37
  496.1 15.6 %all_gather.3 = bf16[128,2048]{1,0:T(8,128)(2,1)S(1)} all-gather(bf16[32,2048]{1,0:T(8,128)(2,1)S(1)} %bitcast.23), channel_id=1, replica_groups=mesh['groups'=2,'tensor'=4,'dp'=4] {'tensor'}, dimensions={0}, use_global_device_ids=true | all-gather | bytes 655360 | tf_op jit(solution)/shard_map/all_gather | solution.py:42
  511.7 15.5 %fusion.13 = f32[7296,128]{0,1:T(8,128)} fusion(bf16[128,2048]{1,0:T(8,128)(2,1)S(1)} %all_gather.3, bf16[2048,7296]{1,0:T(8,128)(2,1)} %concatenate.9), kind=kOutput, calls=%fused_computation.26 | convolution fusion | flops 3825205248 | bytes 34144256 | tf_op jit(solution)/shard_map/dot_general | solution.py:41
  527.3 0.0 all-reduce.4.cloned.1.call-update
  527.3 0.0 reduce-scatter.3.cloned.1.call-start
  527.4 1.2 dynamic-slice
  528.6 13.5 %constant_dynamic-update-slice_fusion.7 = bf16[3584,16384]{1,0:T(8,128)(2,1)} fusion(bf16[3584,2048]{1,0:T(8,128)(2,1)} %param.13), kind=kLoop, calls=%fused_computation.18 | loop fusion | bytes 29360128
  542.1 65.1 %all-reduce.4.cloned.1.call-done = f32[4,4,8,7296]{3,2,1,0:T(8,128)} async-done(((f32[4,4,8,7296]{3,2,1,0:T(8,128)}), f32[4,4,8,7296]{3,2,1,0:T(8,128)}) %all-reduce.4.cloned.1.call-update) | async-done | bytes 3735568
  607.2 1.9 fusion.11
  609.1 0.0 copy-done.3
  609.1 0.2 fusion.4
  609.3 0.0 copy-done.4
  609.3 0.3 fusion.5
  609.7 13.4 %constant_dynamic-update-slice_fusion.6 = bf16[3584,16384]{1,0:T(8,128)(2,1)} fusion(bf16[3584,16384]{1,0:T(8,128)(2,1)} %constant_dynamic-update-slice_fusion.7, bf16[3584,2048]{1,0:T(8,128)(2,1)} %copy-done.1), kind=kLoop, calls=%fused_computation.17 | loop fusion | bytes 29360128
  623.1 0.0 copy-start.5
  623.1 0.0 copy-start.2
  623.1 13.5 %constant_dynamic-update-slice_fusion.5 = bf16[3584,16384]{1,0:T(8,128)(2,1)} fusion(bf16[3584,16384]{1,0:T(8,128)(2,1)} %constant_dynamic-update-slice_fusion.6, bf16[3584,2048]{1,0:T(8,128)(2,1)} %collective-permute-done.1), kind=kLoop, calls=%fused_computation.16 | loop fusion | bytes 29360128
  636.6 0.0 collective-permute-done.2
  636.6 13.4 %constant_dynamic-update-slice_fusion.4 = bf16[3584,16384]{1,0:T(8,128)(2,1)} fusion(bf16[3584,16384]{1,0:T(8,128)(2,1)} %constant_dynamic-update-slice_fusion.5, bf16[3584,2048]{1,0:T(8,128)(2,1)} %collective-permute-done.2), kind=kLoop, calls=%fused_computation.15 | loop fusion | bytes 29360128
  650.0 13.4 %constant_dynamic-update-slice_fusion.3 = bf16[3584,16384]{1,0:T(8,128)(2,1)} fusion(bf16[3584,16384]{1,0:T(8,128)(2,1)} %constant_dynamic-update-slice_fusion.4, bf16[3584,2048]{1,0:T(8,128)(2,1)} %param.13), kind=kLoop, calls=%fused_computation.14 | loop fusion | bytes 29360128
  663.4 13.4 %constant_dynamic-update-slice_fusion.2 = bf16[3584,16384]{1,0:T(8,128)(2,1)} fusion(bf16[3584,16384]{1,0:T(8,128)(2,1)} %constant_dynamic-update-slice_fusion.3, bf16[3584,2048]{1,0:T(8,128)(2,1)} %copy-done.1), kind=kLoop, calls=%fused_computation.13 | loop fusion | bytes 29360128
  676.8 13.4 %constant_dynamic-update-slice_fusion.1 = bf16[3584,16384]{1,0:T(8,128)(2,1)} fusion(bf16[3584,16384]{1,0:T(8,128)(2,1)} %constant_dynamic-update-slice_fusion.2, bf16[3584,2048]{1,0:T(8,128)(2,1)} %collective-permute-done.1), kind=kLoop, calls=%fused_computation.12 | loop fusion | bytes 29360128
  690.2 13.4 %constant_dynamic-update-slice_fusion = bf16[3584,16384]{1,0:T(8,128)(2,1)} fusion(bf16[3584,16384]{1,0:T(8,128)(2,1)} %constant_dynamic-update-slice_fusion.1, bf16[3584,2048]{1,0:T(8,128)(2,1)} %collective-permute-done.2), kind=kLoop, calls=%fused_computation.11 | loop fusion | bytes 29360128 | tf_op jit(solution)/shard_map/jit(_roll_dynamic)/concatenate | solution.py:17
  703.7 21.7 %fusion = f32[32,8192]{1,0:T(8,128)} fusion(bf16[32,3584]{1,0:T(8,128)(2,1)S(1)} %fusion.5, bf16[3584,16384]{1,0:T(8,128)(2,1)} %constant_dynamic-update-slice_fusion, s32[]{:T(128)S(6)} %select_n.14), kind=kOutput, calls=%fused_computation | convolution fusion | flops 1879048192 | bytes 59998212 | tf_op jit(solution)/shard_map/dot_general | solution.py:71
  725.3 0.0 reduce-scatter.3.cloned.1.call-update
  725.4 0.0 copy-done.5
  725.4 0.6 dynamic-slice.2
  726.6 0.0 copy-done.2
  726.6 0.2 fusion.12
  726.8 19.3 %all-reduce.1 = f32[32,64]{1,0:T(8,128)S(1)} all-reduce(f32[32,64]{1,0:T(8,128)S(1)} %fusion.12), channel_id=4, replica_groups=mesh['groups'=2,'tensor'=4,'dp'=4] {'tensor'}, use_global_device_ids=true, to_apply=%region_2.3.clone | all-reduce | flops 2048 | bytes 16384
  746.1 0.0 copy-done
  746.1 0.5 convolution_multiply_fusion
  746.7 6.8 reduce-scatter.3.cloned.1.call-done
  753.5 1.6 add_convert_fusion
Async XLA Ops:
  6.5 739.6 %copy-start = (bf16[64,8192]{1,0:T(8,128)(2,1)S(1)}, bf16[64,8192]{1,0:T(8,128)(2,1)}, u32[]{:S(2)}) copy-start(bf16[64,8192]{1,0:T(8,128)(2,1)} %param.19) | copy-start | bytes 3145732
  6.5 602.6 %copy-start.3 = (bf16[64,3584]{1,0:T(8,128)(2,1)S(1)}, bf16[64,3584]{1,0:T(8,128)(2,1)}, u32[]{:S(2)}) copy-start(bf16[64,3584]{1,0:T(8,128)(2,1)} %param.15) | copy-start | bytes 1376260
  6.5 602.8 %copy-start.4 = (bf16[64,3584]{1,0:T(8,128)(2,1)S(1)}, bf16[64,3584]{1,0:T(8,128)(2,1)}, u32[]{:S(2)}) copy-start(bf16[64,3584]{1,0:T(8,128)(2,1)} %param.17) | copy-start | bytes 1376260
  6.5 161.1 %collective-permute-start = (bf16[3584,2048]{1,0:T(8,128)(2,1)}, bf16[3584,2048]{1,0:T(8,128)(2,1)S(1)}, u32[]{:S(2)}, u32[]{:S(2)}) collective-permute-start(bf16[3584,2048]{1,0:T(8,128)(2,1)} %param.13), channel_id=1, source_target_pairs={{0,3},{1,0},{2,1},{3,2},{4,7},{5,4},{6,5},{7,6},{8,11},{9,8},{10,9... | collective-permute-start | bytes 44040200 | tf_op jit(solution)/shard_map/ppermute | solution.py:14
  167.6 5.2 copy-start.1
  172.9 160.2 %collective-permute-start.1 = (bf16[3584,2048]{1,0:T(8,128)(2,1)S(1)}, bf16[3584,2048]{1,0:T(8,128)(2,1)}, u32[]{:S(2)}, u32[]{:S(2)}) collective-permute-start(bf16[3584,2048]{1,0:T(8,128)(2,1)S(1)} %collective-permute-done), channel_id=1, source_target_pairs={{0,3},{1,0},{2,1},{3,2},{4,7},{5,4},{6,5},{7,6},{8,11},{9,8},{10,9... | collective-permute-start | bytes 44040200 | tf_op jit(solution)/shard_map/ppermute | solution.py:14
  333.0 303.5 %collective-permute-start.2 = (bf16[3584,2048]{1,0:T(8,128)(2,1)}, bf16[3584,2048]{1,0:T(8,128)(2,1)}, u32[]{:S(2)}, u32[]{:S(2)}) collective-permute-start(bf16[3584,2048]{1,0:T(8,128)(2,1)} %collective-permute-done.1), channel_id=1, source_target_pairs={{0,3},{1,0},{2,1},{3,2},{4,7},{5,4},{6,5},{7,6},{8,11},{9,8},{10,9... | collective-permute-start | bytes 44040200 | tf_op jit(solution)/shard_map/ppermute | solution.py:14
  335.1 161.0 %all-to-all-start = ((bf16[8,4,2048]{2,0,1:T(8,128)(2,1)}), bf16[8,4,2048]{2,0,1:T(8,128)(2,1)S(1)}, u32[]{:S(2)}, u32[]{:S(2)}) async-start(bf16[8,4,2048]{2,0,1:T(8,128)(2,1)} %bitcast.24), calls=%async_computation | async-start | bytes 262144 | tf_op jit(solution)/shard_map/all_to_all | solution.py:37
  338.4 268.8 %all-reduce.4.cloned.1.call-start = ((), (), s32[]{:S(2)}) async-start(), calls=%async_computation.3 | async-start | bytes 7471104
  527.3 226.2 %reduce-scatter.3.cloned.1.call-start = ((), (), s32[]{:S(2)}) async-start(), calls=%async_computation.2 | async-start | bytes 1310720 | tf_op jit(solution)/shard_map/reduce_scatter | solution.py:74
  623.1 102.3 %copy-start.5 = (u32[32]{0:T(128)S(1)}, u32[32]{0:T(128)}, u32[]{:S(2)}) copy-start(u32[32]{0:T(128)} %constant.41) | copy-start | bytes 388
  623.1 103.5 %copy-start.2 = (bf16[3584,64]{0,1:T(8,128)(2,1)S(1)}, bf16[3584,64]{0,1:T(8,128)(2,1)}, u32[]{:S(2)}) copy-start(bf16[3584,64]{0,1:T(8,128)(2,1)} %param.18) | copy-start | bytes 1376260
Sparse Core Ops, SparseCore 0:
  527.4 79.7 all-reduce.3
  725.5 27.9 reduce-scatter.2
